TPU v7x, 32 devices: a whole 2x2x4 slice. The times are simulated.
32 devices in a mesh: gx: 8 (over y, x, core), gy: 4 (over z).
Axes of the slice: x: 2, y: 2, z: 4, core: 2. Of those that a mesh axis runs over, the one named last changes fastest.
Arguments:
- tracer_amounts: bfloat16 [2, 512, 512, 128], P(None, ('gx', 'gy')), may hold values from 0.099609375 to 3
- zonal_transit_ratio: float32 [2, 512, 512], P(None, 'gx', 'gy'), may hold values from -0.5 to 0.5
- meridional_transit_ratio: float32 [2, 512, 512], P(None, 'gx', 'gy'), may hold values from -0.45 to 0.45
- moisture_ratio: float32 [2, 512, 512], P(None, 'gx', 'gy'), may hold values from 0.2 to 0.9
- stratum_depths: float32 [2, 512, 512], P(None, 'gx', 'gy'), may hold values from 0.5 to 2
- sun_elevation_factor: float32 [512, 512], P('gx', 'gy'), may hold values from 0.2 to 1
- thermal_anomaly: float32 [2, 512, 512], P(None, 'gx', 'gy'), may hold values from -6 to 6
- particle_class_map: int32 [512, 512], P(('gx', 'gy')), may hold values from 0 to 7
- ground_cover_kind: int32 [512, 512], P(('gx', 'gy')), may hold values from 0 to 23
- arid_extinction_table: bfloat16 [128, 64], replicated, may hold values from 0 to 0.015625
- swelling_factors: bfloat16 [128, 64], replicated, may hold values from 0 to 0.00390625
- settling_velocities: float32 [24, 128], replicated, may hold values from 0.05 to 2
- arriving_irradiance: float32 [4], replicated, may hold values from 0.5 to 2
Outputs:
- updated_tracer_amounts: float32 [2, 512, 512, 128], P(None, ('gx', 'gy'))
- updated_thermal_anomaly: float32 [2, 512, 512], P(None, 'gx', 'gy')
All inputs are finite; a program needn't handle non-finite values.
Results may differ from a plain program's by a relative error of at most 0.00075.
Values may be sent and summed in bfloat16 or wider, within the bound.
A program may use at most 128 MiB of HBM per device.

v0:
```python
import jax
import jax.numpy as jnp
from jax import lax
from jax.sharding import PartitionSpec as P

SUB = 3
NBIN = 8
NW = 4
SPREAD_FACTOR = 0.2


def padded(cells, sides, width):
    for axis, dim in sides:
        count = lax.axis_size(axis)
        ends = count - 1
        head = lax.slice_in_dim(cells, 0, width, axis=dim)
        tail = lax.slice_in_dim(cells, cells.shape[dim] - width, cells.shape[dim], axis=dim)
        cells = jnp.concatenate(
            [
                lax.ppermute(tail, axis, [(i, (i + 1) % count) for i in range(ends)]),
                cells,
                lax.ppermute(head, axis, [((i + 1) % count, i) for i in range(ends)]),
            ],
            axis=dim,
        )
    return cells


def upwind(tracer, west_side, east_side, south_side, north_side, east_courant, north_courant):
    return (
        tracer
        - jnp.maximum(east_courant, 0.0) * (tracer - west_side)
        - jnp.minimum(east_courant, 0.0) * (east_side - tracer)
        - jnp.maximum(north_courant, 0.0) * (tracer - south_side)
        - jnp.minimum(north_courant, 0.0) * (north_side - tracer)
    )


def advance(widened, east_courant, north_courant):
    inner = widened[:, 1:-1]
    padded_y = jnp.pad(inner, ((0, 0), (0, 0), (1, 1), (0, 0)))
    return upwind(
        inner,
        widened[:, :-2],
        widened[:, 2:],
        padded_y[:, :, :-2],
        padded_y[:, :, 2:],
        east_courant,
        north_courant,
    )


def radiate(optical, cosine, sunlight):
    layers_count = optical.shape[0]
    wavelengths = optical.shape[1] // 2
    weights = sunlight.reshape((wavelengths,) + (1,) * (optical.ndim - 2))
    overhead = jnp.zeros_like(optical[0, :wavelengths])
    layers = [None] * layers_count
    for height in reversed(range(layers_count)):
        transmitted = jnp.exp(-overhead / cosine)
        layers[height] = cosine * jnp.sum(
            weights * optical[height, wavelengths:] * transmitted, axis=0
        )
        overhead = overhead + optical[height, :wavelengths]
    return jnp.stack(layers)


def per_device(
    tracer_amounts,
    zonal_transit_ratio,
    meridional_transit_ratio,
    moisture_ratio,
    stratum_depths,
    sun_elevation_factor,
    thermal_anomaly,
    particle_class_map,
    ground_cover_kind,
    arid_extinction_table,
    swelling_factors,
    settling_velocities,
    arriving_irradiance,
):
    tier_pile = thermal_anomaly.shape[0]
    strip_width = tracer_amounts.shape[1]
    species_count = tracer_amounts.shape[3]
    warmed_fringe_points = padded(
        thermal_anomaly.astype(jnp.bfloat16), (("gx", 1), ("gy", 2)), 1
    ).astype(thermal_anomaly.dtype)
    second_difference_map = (
        warmed_fringe_points[:, 2:, 1:-1]
        + warmed_fringe_points[:, :-2, 1:-1]
        + warmed_fringe_points[:, 1:-1, 2:]
        + warmed_fringe_points[:, 1:-1, :-2]
        - 4.0 * thermal_anomaly
    )
    fields = jnp.concatenate(
        [zonal_transit_ratio, meridional_transit_ratio, moisture_ratio, stratum_depths], axis=0
    )
    relayed = lax.all_to_all(fields, "gy", split_axis=1, concat_axis=2, tiled=True)
    moisture = relayed[2 * tier_pile : 3 * tier_pile]
    layer_depth = relayed[3 * tier_pile : 4 * tier_pile]
    widened = padded(tracer_amounts, ((("gx", "gy"), 1),), SUB).astype(jnp.float32)
    wind_rims = padded(relayed[: 2 * tier_pile], ((("gx", "gy"), 1),), SUB)
    span_width = strip_width + 2 * SUB
    first_column = lax.axis_index(("gx", "gy")) * strip_width - SUB
    grid_width = strip_width * lax.axis_size(("gx", "gy"))
    column_index = first_column + lax.iota(jnp.int32, span_width)
    inside = ((column_index >= 0) & (column_index < grid_width)).astype(jnp.float32)
    tracer = widened
    for substep in range(SUB):
        lower_edge = substep + 1
        upper_edge = span_width - substep - 1
        east_courant = wind_rims[:tier_pile, lower_edge:upper_edge][..., None]
        north_courant = wind_rims[tier_pile:, lower_edge:upper_edge][..., None]
        tracer = (
            advance(tracer, east_courant, north_courant)
            * inside[lower_edge:upper_edge][None, :, None, None]
        )
    land_count = settling_velocities.shape[0]
    one_hot = (ground_cover_kind[..., None] == lax.iota(jnp.int32, land_count)).astype(jnp.float32)
    loss_rate = jnp.dot(
        one_hot.reshape(-1, land_count), settling_velocities, precision=lax.Precision.HIGHEST
    ).reshape(strip_width, -1, species_count)
    loss_rate = loss_rate / layer_depth[0][..., None]
    updated_tracer_amounts = jnp.concatenate(
        [(tracer[0] / (1.0 + loss_rate))[None], tracer[1:]], axis=0
    )
    rounded = updated_tracer_amounts.astype(jnp.bfloat16)
    optics_table = jnp.concatenate([arid_extinction_table, swelling_factors], axis=1)
    projected = jnp.einsum(
        "lxys,sq->lqxy", rounded, optics_table, preferred_element_type=jnp.float32
    )
    projected = projected.reshape(tier_pile, 2, NBIN, 2 * NW, strip_width, -1)
    growth = moisture / (1.0 - moisture)
    combined = projected[:, 0] + growth[:, None, None] * projected[:, 1]
    bin_mask = (particle_class_map[None] == lax.iota(jnp.int32, NBIN)[:, None, None]).astype(
        jnp.float32
    )
    optical = jnp.sum(combined * bin_mask[None, :, None], axis=1) * layer_depth[:, None]
    payload = optical.reshape(tier_pile * 2 * NW, strip_width, -1)
    returned = lax.all_to_all(payload, "gy", split_axis=2, concat_axis=1, tiled=True)
    warming_tendency = radiate(
        returned.reshape(tier_pile, 2 * NW, returned.shape[1], returned.shape[2]),
        sun_elevation_factor,
        arriving_irradiance,
    )
    updated_thermal_anomaly = (
        thermal_anomaly + SPREAD_FACTOR * second_difference_map + warming_tendency
    )
    return (updated_tracer_amounts, updated_thermal_anomaly)


def solution(mesh):
    return jax.shard_map(
        per_device,
        mesh=mesh,
        in_specs=(
            P(None, ("gx", "gy"), None, None),
            P(None, "gx", "gy"),
            P(None, "gx", "gy"),
            P(None, "gx", "gy"),
            P(None, "gx", "gy"),
            P("gx", "gy"),
            P(None, "gx", "gy"),
            P(("gx", "gy"), None),
            P(("gx", "gy"), None),
            P(),
            P(),
            P(),
            P(),
        ),
        out_specs=(P(None, ("gx", "gy"), None, None), P(None, "gx", "gy")),
        check_vma=False,
    )
```

profile of v0, /device:TPU:3, one launch (start us, length us, event | category | flops | bytes accessed | tf_op | source)
XLA Modules:
  0.0 168.0 jit_solution(12056350276605661121)
XLA Ops:
  0.6 0.9 copy.36
  1.5 0.9 copy.37
  2.4 0.9 copy.38
  3.3 0.9 copy.39
  4.2 0.8 pad_maximum_fusion.1
  5.1 4.6 %all-to-all-start = ((f32[8,64,128]{2,0,1:T(8,128)}), f32[8,64,128]{2,0,1:T(8,128)S(1)}, u32[]{:S(2)}, u32[]{:S(2)}) async-start(f32[8,64,128]{2,0,1:T(8,128)} %pad_maximum_fusion.1), calls=%async_computation | async-start | bytes 524288 | tf_op jit(solution)/shard_map/all_to_all | solution.py:99
  9.7 2.4 %fusion.48 = (bf16[2,3,512,128]{3,2,1,0:T(8,128)(2,1)}, bf16[2,3,512,128]{3,2,1,0:T(8,128)(2,1)S(1)}) fusion(bf16[2,16,512,128]{3,2,1,0:T(8,128)(2,1)} %param.13), kind=kLoop, calls=%fused_computation.92 | loop fusion | bytes 3145728 | tf_op jit(solution)/shard_map/slice | solution.py:17
  12.0 3.4 %collective-permute-start = (bf16[2,3,512,128]{3,2,1,0:T(8,128)(2,1)}, bf16[2,3,512,128]{3,2,1,0:T(8,128)(2,1)S(1)}, u32[]{:S(2)}, u32[]{:S(2)}) collective-permute-start(bf16[2,3,512,128]{3,2,1,0:T(8,128)(2,1)} %get-tuple-element.4), channel_id=1, source_target_pairs={{0,1},{1,2},{2,3},{3,4},{4,5},{5,6},{6,7},{7,8},{8,9},{9,10},{10,1... | collective-permute-start | bytes 2359304 | tf_op jit(solution)/shard_map/ppermute | solution.py:20
  15.4 4.8 %collective-permute-start.1 = (bf16[2,3,512,128]{3,2,1,0:T(8,128)(2,1)S(1)}, bf16[2,3,512,128]{3,2,1,0:T(8,128)(2,1)S(1)}, u32[]{:S(2)}, u32[]{:S(2)}) collective-permute-start(bf16[2,3,512,128]{3,2,1,0:T(8,128)(2,1)S(1)} %get-tuple-element.5), channel_id=1, source_target_pairs={{1,0},{2,1},{3,2},{4,3},{5,4},{6,5},{7,6},{8,7},{9,8},{10,9},{11,1... | collective-permute-start | bytes 2359304 | tf_op jit(solution)/shard_map/ppermute | solution.py:22
  20.2 0.1 slice.167
  20.3 0.1 slice.175
  20.4 0.1 slice.183
  20.5 0.8 convert_element_type.31
  21.3 0.8 fusion.30
  22.1 0.2 copy.54
  22.3 0.7 fusion.49
  23.0 0.1 slice.158
  23.1 0.6 fusion.50
  23.7 1.9 %collective-permute-start.2 = (f32[4,3,512]{2,1,0:T(4,128)}, f32[4,3,512]{2,1,0:T(4,128)S(1)}, u32[]{:S(2)}, u32[]{:S(2)}) collective-permute-start(f32[4,3,512]{2,1,0:T(4,128)} %get-tuple-element.20), channel_id=1, source_target_pairs={{0,1},{1,2},{2,3},{3,4},{4,5},{5,6},{6,7},{7,8},{8,9},{9,10},{10,1... | collective-permute-start | bytes 73736 | tf_op jit(solution)/shard_map/ppermute | solution.py:20
  25.6 5.4 %collective-permute-start.3 = (f32[4,3,512]{2,1,0:T(4,128)}, f32[4,3,512]{2,1,0:T(4,128)S(1)}, u32[]{:S(2)}, u32[]{:S(2)}) collective-permute-start(f32[4,3,512]{2,1,0:T(4,128)} %get-tuple-element.21), channel_id=1, source_target_pairs={{1,0},{2,1},{3,2},{4,3},{5,4},{6,5},{7,6},{8,7},{9,8},{10,9},{11,1... | collective-permute-start | bytes 73736 | tf_op jit(solution)/shard_map/ppermute | solution.py:22
  31.0 0.9 slice.197
  31.9 0.6 subtract_divide_fusion
  32.6 1.5 max.43
  34.0 0.6 max.45
  34.7 0.6 min.43
  35.3 0.7 min.45
  36.0 0.7 mul.235
  36.6 17.5 %collective-permute-done.2 = f32[4,3,512]{2,1,0:T(4,128)S(1)} collective-permute-done((f32[4,3,512]{2,1,0:T(4,128)}, f32[4,3,512]{2,1,0:T(4,128)S(1)}, u32[]{:S(2)}, u32[]{:S(2)}) %collective-permute-start.2) | collective-permute-done | bytes 24608 | tf_op jit(solution)/shard_map/ppermute | solution.py:20
  54.1 0.8 collective-permute-done.3
  55.0 0.7 slice_maximum_fusion.3
  55.7 0.7 slice_maximum_fusion.1
  56.4 3.5 %maximum_convert_fusion = f32[2,22,512,128]{3,2,1,0:T(8,128)S(1)} fusion(bf16[2,3,512,128]{3,2,1,0:T(8,128)(2,1)S(1)} %collective-permute-done.1, bf16[2,16,512,128]{3,2,1,0:T(8,128)(2,1)} %param.13, bf16[2,3,512,128]{3,2,1,0:T(8,128)(2,1)S(1)} %collective-permute-done), kind=kLoop, calls=%fused_computation.28 | loop fusion | flops 8650752 | bytes 17301504 | tf_op jit(solution)/shard_map/convert_element_type | solution.py:102
  60.0 4.7 %slice.203 = f32[2,20,512,128]{3,2,1,0:T(8,128)} slice(f32[2,22,512,128]{3,2,1,0:T(8,128)S(1)} %maximum_convert_fusion), slice={[0:2], [1:21], [0:512], [0:128]} | slice | bytes 20971520 | tf_op jit(solution)/shard_map/slice | solution.py:40
  64.7 15.3 %fusion.4 = f32[2,20,512,128]{3,2,1,0:T(8,128)} fusion(f32[2,20,512,128]{3,2,1,0:T(8,128)} %slice.203, f32[2,22,512,128]{3,2,1,0:T(8,128)S(1)} %maximum_convert_fusion, f32[20]{0:T(128)S(1)} %slice.167, f32[2,20,512]{2,1,0:T(8,128)S(1)} %copy-done.3, f32[2,20,512]{2,1,0:T(8,128)S(1)} %copy-done.4, f32[2,20,512]{2,1,0:T(8,128)S(1)} %get-tuple-element.17, ...), kind=kLoop, calls=%fused_computation.5 | loop fusion | flops 34078720 | bytes 42270800 | tf_op jit(solution)/shard_map/mul | solution.py:116
  80.1 3.7 %slice-done = f32[2,18,512,128]{3,2,1,0:T(8,128)S(1)} async-done(((f32[2,20,512,128]{3,2,1,0:T(8,128)}), f32[2,18,512,128]{3,2,1,0:T(8,128)S(1)}, s32[]{:S(2)}) %slice-start) | async-done | bytes 9437208 | tf_op jit(solution)/shard_map/slice | solution.py:40
  83.7 13.3 %fusion.11 = f32[2,18,512,128]{3,2,1,0:T(8,128)S(1)} fusion(f32[2,18,512,128]{3,2,1,0:T(8,128)S(1)} %slice-done, f32[2,20,512,128]{3,2,1,0:T(8,128)} %fusion.4, f32[18]{0:T(128)S(1)} %slice.175, f32[2,18,512]{2,1,0:T(8,128)} %get-tuple-element.14, f32[2,18,512]{2,1,0:T(8,128)} %get-tuple-element.15, f32[2,18,512]{2,1,0:T(8,128)S(1)} %get-tuple-element.13, ...), kind=kLoop, calls=%fused_computation.14 | loop fusion | flops 30670848 | bytes 38043720 | tf_op jit(solution)/shard_map/mul | solution.py:116
  97.0 0.6 slice.216
  97.6 0.2 copy-done.7
  97.9 10.9 %fusion.18 = f32[2,16,512,128]{3,2,1,0:T(8,128)} fusion(f32[2,16,512,128]{3,2,1,0:T(8,128)S(1)} %slice.216, f32[2,18,512,128]{3,2,1,0:T(8,128)S(1)} %fusion.11, f32[16]{0:T(128)S(1)} %slice.183, f32[2,16,512]{2,1,0:T(8,128)S(1)} %copy-done.10, f32[2,16,512]{2,1,0:T(8,128)S(1)} %copy-done.8, f32[2,16,512]{2,1,0:T(8,128)S(1)} %copy-done.9, ...), kind=kLoop, calls=%fused_computation.23 | loop fusion | flops 27262976 | bytes 33816640 | tf_op jit(solution)/shard_map/mul | solution.py:116
  108.8 3.4 %copy-done.2 = f32[2,16,512,128]{3,2,1,0:T(8,128)S(1)} copy-done((f32[2,16,512,128]{3,2,1,0:T(8,128)S(1)}, f32[2,16,512,128]{3,2,1,0:T(8,128)}, u32[]{:S(2)}) %copy-start.2) | copy-done | bytes 8388632
  112.2 6.7 %fusion.26 = f32[1,16,512,128]{3,2,1,0:T(8,128)} fusion(f32[2,16,512,128]{3,2,1,0:T(8,128)S(1)} %copy-done.2, f32[16,512]{1,0:T(8,128)S(1)} %bitcast.93, s32[16,512]{1,0:T(8,128)} %param.21, f32[24,128]{1,0:T(8,128)S(1)} %copy-done), kind=kOutput, calls=%fused_computation.37 | convolution fusion | flops 305332224 | bytes 8466432 | tf_op jit(solution)/shard_map/dot_general | solution.py:121
  118.9 3.5 %pad_maximum_fusion = f32[2,16,512,128]{3,2,1,0:T(8,128)S(1)} fusion(f32[1,16,512,128]{3,2,1,0:T(8,128)S(1)} %slice-done.1, f32[1,16,512,128]{3,2,1,0:T(8,128)} %fusion.26), kind=kLoop, calls=%fused_computation.27 | loop fusion | flops 2097152 | bytes 16777216 | tf_op jit(solution)/shard_map/concatenate | solution.py:125
  122.4 1.3 fusion.27
  123.7 2.1 %copy-done.1 = f32[2,16,512,128]{3,2,1,0:T(8,128)} copy-done((f32[2,16,512,128]{3,2,1,0:T(8,128)}, f32[2,16,512,128]{3,2,1,0:T(8,128)S(1)}, u32[]{:S(2)}) %copy-start.1) | copy-done | bytes 8388632
  125.8 1.4 fusion.24
  127.2 0.1 broadcast_multiply_fusion
  127.3 0.3 copy.43
  127.6 3.6 %copy.44 = f32[16,16,512]{1,0,2:T(8,128)} copy(f32[16,16,512]{2,1,0:T(8,128)S(1)} %bitcast.85) | data formatting | bytes 1048576 | tf_op jit(solution)/shard_map/mul | solution.py:139
  131.2 4.6 %reshape.118 = f32[4,1,32768]{2,1,0:T(1,128)} reshape(f32[512,16,16]{2,1,0:T(8,128)} %bitcast.83) | data formatting | bytes 1048576
  135.9 3.5 %all-to-all-start.1 = ((f32[4,1,32768]{2,1,0:T(1,128)}), f32[4,1,32768]{2,1,0:T(1,128)S(1)}, u32[]{:S(2)}, u32[]{:S(2)}) async-start(f32[4,1,32768]{2,1,0:T(1,128)} %reshape.118), calls=%async_computation.1 | async-start | bytes 1048576 | tf_op jit(solution)/shard_map/all_to_all | solution.py:141
  139.4 4.2 %collective-permute-start.4 = (bf16[2,1,128]{2,1,0:T(2,128)(2,1)S(1)}, bf16[2,1,128]{2,1,0:T(2,128)(2,1)S(1)}, u32[]{:S(2)}, u32[]{:S(2)}) collective-permute-start(bf16[2,1,128]{2,1,0:T(2,128)(2,1)S(1)} %get-tuple-element.26), channel_id=1, source_target_pairs={{0,4},{4,8},{8,12},{12,16},{16,20},{20,24},{24,28},{1,5},{5,9},{9,... | collective-permute-start | bytes 1544 | tf_op jit(solution)/shard_map/ppermute | solution.py:20
  143.5 2.1 %collective-permute-start.5 = (bf16[2,1,128]{2,1,0:T(2,128)(2,1)S(1)}, bf16[2,1,128]{2,1,0:T(2,128)(2,1)S(1)}, u32[]{:S(2)}, u32[]{:S(2)}) collective-permute-start(bf16[2,1,128]{2,1,0:T(2,128)(2,1)S(1)} %get-tuple-element.27), channel_id=1, source_target_pairs={{4,0},{8,4},{12,8},{16,12},{20,16},{24,20},{28,24},{5,1},{9,5},{13... | collective-permute-start | bytes 1544 | tf_op jit(solution)/shard_map/ppermute | solution.py:22
  145.7 3.7 %collective-permute-done.5 = bf16[2,1,128]{2,1,0:T(2,128)(2,1)S(1)} collective-permute-done((bf16[2,1,128]{2,1,0:T(2,128)(2,1)S(1)}, bf16[2,1,128]{2,1,0:T(2,128)(2,1)S(1)}, u32[]{:S(2)}, u32[]{:S(2)}) %collective-permute-start.5) | collective-permute-done | bytes 544 | tf_op jit(solution)/shard_map/ppermute | solution.py:22
  149.4 0.1 fusion.51
  149.4 3.9 %collective-permute-start.6 = (bf16[2,66,1]{2,1,0:T(8,128)(2,1)S(1)}, bf16[2,66,1]{2,1,0:T(8,128)(2,1)S(1)}, u32[]{:S(2)}, u32[]{:S(2)}) collective-permute-start(bf16[2,66,1]{2,1,0:T(8,128)(2,1)S(1)} %get-tuple-element.22), channel_id=1, source_target_pairs={{0,1},{1,2},{2,3},{4,5},{5,6},{6,7},{8,9},{9,10},{10,11},{12,13},{... | collective-permute-start | bytes 800 | tf_op jit(solution)/shard_map/ppermute | solution.py:20
  153.3 1.3 collective-permute-start.7
  154.7 3.4 %collective-permute-done.7 = bf16[2,66,1]{2,1,0:T(8,128)(2,1)S(1)} collective-permute-done((bf16[2,66,1]{2,1,0:T(8,128)(2,1)S(1)}, bf16[2,66,1]{2,1,0:T(8,128)(2,1)S(1)}, u32[]{:S(2)}, u32[]{:S(2)}) %collective-permute-start.7) | collective-permute-done | bytes 296 | tf_op jit(solution)/shard_map/ppermute | solution.py:22
  158.0 0.1 maximum_convert_fusion.1
  158.2 0.5 broadcast.108
  158.7 2.2 %reduce = f32[4,32768]{1,0:T(4,128)S(1)} reduce(f32[4,1,32768]{2,1,0:T(1,128)S(1)} %all-to-all-done.1, f32[]{:T(128)} %broadcast.108), dimensions={1}, to_apply=%all_to_all.25.reduce_sub_computation | reduce | bytes 1048580 | tf_op jit(solution)/shard_map/all_to_all | solution.py:141
  160.8 3.4 %reshape.119 = f32[512,16,16]{2,1,0:T(8,128)} reshape(f32[4,32768]{1,0:T(4,128)S(1)} %reduce) | data formatting | bytes 1048576
  164.3 2.8 %copy.48 = f32[16,16,4,128]{3,2,1,0:T(4,128)S(1)} copy(f32[16,16,4,128]{1,0,3,2:T(8,128)} %bitcast.84) | data formatting | bytes 1048576 | tf_op jit(solution)/shard_map/all_to_all | solution.py:141
  167.1 0.1 fusion.39
  167.3 0.8 fusion.43
  (48 shorter events, 0.3 us)
Async XLA Ops:
  0.6 108.2 %copy-start = (f32[24,128]{1,0:T(8,128)S(1)}, f32[24,128]{1,0:T(8,128)}, u32[]{:S(2)}) copy-start(f32[24,128]{1,0:T(8,128)} %param.24) | copy-start | bytes 36868
  5.1 17.0 %all-to-all-start = ((f32[8,64,128]{2,0,1:T(8,128)}), f32[8,64,128]{2,0,1:T(8,128)S(1)}, u32[]{:S(2)}, u32[]{:S(2)}) async-start(f32[8,64,128]{2,0,1:T(8,128)} %pad_maximum_fusion.1), calls=%async_computation | async-start | bytes 524288 | tf_op jit(solution)/shard_map/all_to_all | solution.py:99
  12.0 44.4 %collective-permute-start = (bf16[2,3,512,128]{3,2,1,0:T(8,128)(2,1)}, bf16[2,3,512,128]{3,2,1,0:T(8,128)(2,1)S(1)}, u32[]{:S(2)}, u32[]{:S(2)}) collective-permute-start(bf16[2,3,512,128]{3,2,1,0:T(8,128)(2,1)} %get-tuple-element.4), channel_id=1, source_target_pairs={{0,1},{1,2},{2,3},{3,4},{4,5},{5,6},{6,7},{7,8},{8,9},{9,10},{10,1... | collective-permute-start | bytes 2359304 | tf_op jit(solution)/shard_map/ppermute | solution.py:20
  15.4 41.1 %collective-permute-start.1 = (bf16[2,3,512,128]{3,2,1,0:T(8,128)(2,1)S(1)}, bf16[2,3,512,128]{3,2,1,0:T(8,128)(2,1)S(1)}, u32[]{:S(2)}, u32[]{:S(2)}) collective-permute-start(bf16[2,3,512,128]{3,2,1,0:T(8,128)(2,1)S(1)} %get-tuple-element.5), channel_id=1, source_target_pairs={{1,0},{2,1},{3,2},{4,3},{5,4},{6,5},{7,6},{8,7},{9,8},{10,9},{11,1... | collective-permute-start | bytes 2359304 | tf_op jit(solution)/shard_map/ppermute | solution.py:22
  23.7 30.5 %collective-permute-start.2 = (f32[4,3,512]{2,1,0:T(4,128)}, f32[4,3,512]{2,1,0:T(4,128)S(1)}, u32[]{:S(2)}, u32[]{:S(2)}) collective-permute-start(f32[4,3,512]{2,1,0:T(4,128)} %get-tuple-element.20), channel_id=1, source_target_pairs={{0,1},{1,2},{2,3},{3,4},{4,5},{5,6},{6,7},{7,8},{8,9},{9,10},{10,1... | collective-permute-start | bytes 73736 | tf_op jit(solution)/shard_map/ppermute | solution.py:20
  25.6 29.3 %collective-permute-start.3 = (f32[4,3,512]{2,1,0:T(4,128)}, f32[4,3,512]{2,1,0:T(4,128)S(1)}, u32[]{:S(2)}, u32[]{:S(2)}) collective-permute-start(f32[4,3,512]{2,1,0:T(4,128)} %get-tuple-element.21), channel_id=1, source_target_pairs={{1,0},{2,1},{3,2},{4,3},{5,4},{6,5},{7,6},{8,7},{9,8},{10,9},{11,1... | collective-permute-start | bytes 73736 | tf_op jit(solution)/shard_map/ppermute | solution.py:22
  60.0 4.7 %copy-start.3 = (f32[2,20,512]{2,1,0:T(8,128)S(1)}, f32[2,20,512]{2,1,0:T(8,128)}, u32[]{:S(2)}) copy-start(f32[2,20,512]{2,1,0:T(8,128)} %get-tuple-element.18) | copy-start | bytes 245764
  60.0 4.7 %copy-start.4 = (f32[2,20,512]{2,1,0:T(8,128)S(1)}, f32[2,20,512]{2,1,0:T(8,128)}, u32[]{:S(2)}) copy-start(f32[2,20,512]{2,1,0:T(8,128)} %get-tuple-element.19) | copy-start | bytes 245764
  80.0 3.7 %slice-start = ((f32[2,20,512,128]{3,2,1,0:T(8,128)}), f32[2,18,512,128]{3,2,1,0:T(8,128)S(1)}, s32[]{:S(2)}) async-start(f32[2,20,512,128]{3,2,1,0:T(8,128)} %fusion.4), calls=%async_computation.2 | async-start | bytes 18874368 | tf_op jit(solution)/shard_map/slice | solution.py:40
  97.0 0.8 copy-start.7
  97.0 0.9 copy-start.8
  97.0 0.9 copy-start.9
  97.0 0.9 copy-start.10
  108.8 3.4 %copy-start.2 = (f32[2,16,512,128]{3,2,1,0:T(8,128)S(1)}, f32[2,16,512,128]{3,2,1,0:T(8,128)}, u32[]{:S(2)}) copy-start(f32[2,16,512,128]{3,2,1,0:T(8,128)} %fusion.18) | copy-start | bytes 25165828
  112.2 6.7 %slice-start.1 = ((f32[2,16,512,128]{3,2,1,0:T(8,128)}), f32[1,16,512,128]{3,2,1,0:T(8,128)S(1)}, s32[]{:S(2)}) async-start(f32[2,16,512,128]{3,2,1,0:T(8,128)} %fusion.18), calls=%async_computation.3 | async-start | bytes 8388608 | tf_op jit(solution)/shard_map/slice | solution.py:126
  118.9 3.5 %copy-start.13 = (bf16[128,64]{0,1:T(8,128)(2,1)S(1)}, bf16[128,64]{0,1:T(8,128)(2,1)}, u32[]{:S(2)}) copy-start(bf16[128,64]{0,1:T(8,128)(2,1)} %param.23) | copy-start | bytes 49156
  118.9 3.5 %copy-start.14 = (bf16[128,64]{0,1:T(8,128)(2,1)S(1)}, bf16[128,64]{0,1:T(8,128)(2,1)}, u32[]{:S(2)}) copy-start(bf16[128,64]{0,1:T(8,128)(2,1)} %param.22) | copy-start | bytes 49156
  122.4 3.4 %copy-start.1 = (f32[2,16,512,128]{3,2,1,0:T(8,128)}, f32[2,16,512,128]{3,2,1,0:T(8,128)S(1)}, u32[]{:S(2)}) copy-start(f32[2,16,512,128]{3,2,1,0:T(8,128)S(1)} %pad_maximum_fusion) | copy-start | bytes 25165828
  122.4 3.4 %copy-start.6 = (f32[2,16,512]{2,1,0:T(8,128)S(1)}, f32[2,16,512]{2,1,0:T(8,128)}, u32[]{:S(2)}) copy-start(f32[2,16,512]{2,1,0:T(8,128)} %subtract_divide_fusion) | copy-start | bytes 196612
  125.8 1.4 copy-start.12
  127.2 27.4 %copy-start.5 = (f32[64,128]{1,0:T(8,128)S(1)}, f32[64,128]{1,0:T(8,128)}, u32[]{:S(2)}) copy-start(f32[64,128]{1,0:T(8,128)} %param.18) | copy-start | bytes 98308
  131.2 35.9 %copy-start.15 = (f32[4]{0:T(128)S(1)}, f32[4]{0:T(128)}, u32[]{:S(2)}) copy-start(f32[4]{0:T(128)} %param.25) | copy-start | bytes 52
  131.2 36.0 %copy-start.11 = (f32[2,64,128]{2,1,0:T(8,128)S(1)}, f32[2,64,128]{2,1,0:T(8,128)}, u32[]{:S(2)}) copy-start(f32[2,64,128]{2,1,0:T(8,128)} %param.19) | copy-start | bytes 196612
  135.9 22.3 %all-to-all-start.1 = ((f32[4,1,32768]{2,1,0:T(1,128)}), f32[4,1,32768]{2,1,0:T(1,128)S(1)}, u32[]{:S(2)}, u32[]{:S(2)}) async-start(f32[4,1,32768]{2,1,0:T(1,128)} %reshape.118), calls=%async_computation.1 | async-start | bytes 1048576 | tf_op jit(solution)/shard_map/all_to_all | solution.py:141
  139.4 6.3 %collective-permute-start.4 = (bf16[2,1,128]{2,1,0:T(2,128)(2,1)S(1)}, bf16[2,1,128]{2,1,0:T(2,128)(2,1)S(1)}, u32[]{:S(2)}, u32[]{:S(2)}) collective-permute-start(bf16[2,1,128]{2,1,0:T(2,128)(2,1)S(1)} %get-tuple-element.26), channel_id=1, source_target_pairs={{0,4},{4,8},{8,12},{12,16},{16,20},{20,24},{24,28},{1,5},{5,9},{9,... | collective-permute-start | bytes 1544 | tf_op jit(solution)/shard_map/ppermute | solution.py:20
  143.5 5.8 %collective-permute-start.5 = (bf16[2,1,128]{2,1,0:T(2,128)(2,1)S(1)}, bf16[2,1,128]{2,1,0:T(2,128)(2,1)S(1)}, u32[]{:S(2)}, u32[]{:S(2)}) collective-permute-start(bf16[2,1,128]{2,1,0:T(2,128)(2,1)S(1)} %get-tuple-element.27), channel_id=1, source_target_pairs={{4,0},{8,4},{12,8},{16,12},{20,16},{24,20},{28,24},{5,1},{9,5},{13... | collective-permute-start | bytes 1544 | tf_op jit(solution)/shard_map/ppermute | solution.py:22
  149.4 5.2 %collective-permute-start.6 = (bf16[2,66,1]{2,1,0:T(8,128)(2,1)S(1)}, bf16[2,66,1]{2,1,0:T(8,128)(2,1)S(1)}, u32[]{:S(2)}, u32[]{:S(2)}) collective-permute-start(bf16[2,66,1]{2,1,0:T(8,128)(2,1)S(1)} %get-tuple-element.22), channel_id=1, source_target_pairs={{0,1},{1,2},{2,3},{4,5},{5,6},{6,7},{8,9},{9,10},{10,11},{12,13},{... | collective-permute-start | bytes 800 | tf_op jit(solution)/shard_map/ppermute | solution.py:20
  153.3 4.7 %collective-permute-start.7 = (bf16[2,66,1]{2,1,0:T(8,128)(2,1)S(1)}, bf16[2,66,1]{2,1,0:T(8,128)(2,1)S(1)}, u32[]{:S(2)}, u32[]{:S(2)}) collective-permute-start(bf16[2,66,1]{2,1,0:T(8,128)(2,1)S(1)} %get-tuple-element.23), channel_id=1, source_target_pairs={{1,0},{2,1},{3,2},{5,4},{6,5},{7,6},{9,8},{10,9},{11,10},{13,12},{... | collective-permute-start | bytes 800 | tf_op jit(solution)/shard_map/ppermute | solution.py:22
where the time goes:
time: 169 us; the launch traced here: 168 us
  other arithmetic  56.4 us (33%)
  local copies, waits for them, and re-layouts  42.3 us (25%)
  starting transfers between devices  35 us (21%)
  waiting for transfers between devices  25.3 us (15%)
  matrix products  7.92 us (5%)
    mul x3, other arithmetic, per_device(): advance(tracer, east_courant, north_courant)  39.5 us
    unnamed x39, local copies, waits for them, and re-layouts  17.5 us
    ppermute x4, waiting for transfers between devices, padded(): lax.ppermute(tail, axis, [(i, (i + 1) % count) for i in range(ends)])  17.5 us
    ppermute x4, starting transfers between devices, padded(): lax.ppermute(head, axis, [((i + 1) % count, i) for i in range(ends)])  13.7 us
    ppermute x4, starting transfers between devices, padded(): lax.ppermute(tail, axis, [(i, (i + 1) % count) for i in range(ends)])  13.3 us
    slice x4, local copies, waits for them, and re-layouts, advance(): inner = widened[:, 1:-1]  8.95 us
    ppermute x4, waiting for transfers between devices, padded(): lax.ppermute(head, axis, [((i + 1) % count, i) for i in range(ends)])  7.83 us
    dot_general x1, matrix products, per_device(): jnp.dot(one_hot.reshape(-1, land_count), settling_velocities, precision=l...  6.66 us
  transfers between devices with their start and end apart: 10, of which 4 were waited for; matrix products, arithmetic and copies ran while one was open for 8% of the time, Pallas kernels for 0%

commit v1 on v0

--- a/solution.py
+++ b/solution.py
@@ -138,7 +138,10 @@
     )
     optical = jnp.sum(combined * bin_mask[None, :, None], axis=1) * layer_depth[:, None]
     payload = optical.reshape(tier_pile * 2 * NW, strip_width, -1)
-    returned = lax.all_to_all(payload, "gy", split_axis=2, concat_axis=1, tiled=True)
+    size = lax.axis_size("gy")
+    shards = jnp.stack(jnp.split(payload, size, axis=2), axis=0)
+    shards = lax.all_to_all(shards, "gy", split_axis=0, concat_axis=0)
+    returned = jnp.concatenate(shards, axis=1)
     warming_tendency = radiate(
         returned.reshape(tier_pile, 2 * NW, returned.shape[1], returned.shape[2]),
         sun_elevation_factor,

time: 169 us -> 153 us (0.905)
  local copies, waits for them, and re-layouts: 42.3 us -> 27.3 us
    unnamed x39 -> x37, local copies, waits for them, and re-layouts: 17.5 us -> 9.46 us
    mul x3 -> x2, local copies, waits for them, and re-layouts: 4.58 us -> 0.96 us  [per_device(): jnp.sum(combined * bin_mask[None, :, None], axis=1) * layer_depth[:, None]]
    all_to_all x3 -> x1, local copies, waits for them, and re-layouts: 3.37 us -> 0.04 us  [per_device(): shards = lax.all_to_all(shards, 'gy', split_axis=0, concat_axis=0)]
    all_to_all x1 -> x0, other arithmetic: 2.17 us -> none  [per_device(): lax.all_to_all(payload, 'gy', split_axis=2, concat_axis=1, tiled=True)]
  transfers between devices with their start and end apart: 10 -> 10, of which waited for: 4 -> 4; matrix products, arithmetic and copies ran while one was open for 8% -> 9% of each run, Pallas kernels for 0% -> 0%
where the time goes in v1:
time: 153 us; the launch traced here: 152 us
  other arithmetic  55.1 us (36%)
  starting transfers between devices  34.9 us (23%)
  local copies, waits for them, and re-layouts  27.3 us (18%)
  waiting for transfers between devices  25.5 us (17%)
  matrix products  7.91 us (5%)
    mul x3, other arithmetic, per_device(): advance(tracer, east_courant, north_courant)  39.5 us
    ppermute x4, waiting for transfers between devices, padded(): lax.ppermute(tail, axis, [(i, (i + 1) % count) for i in range(ends)])  17.5 us
    ppermute x4, starting transfers between devices, padded(): lax.ppermute(head, axis, [((i + 1) % count, i) for i in range(ends)])  13.5 us
    ppermute x4, starting transfers between devices, padded(): lax.ppermute(tail, axis, [(i, (i + 1) % count) for i in range(ends)])  13.3 us
    unnamed x37, local copies, waits for them, and re-layouts  9.46 us
    slice x4, local copies, waits for them, and re-layouts, advance(): inner = widened[:, 1:-1]  8.95 us
    ppermute x4, waiting for transfers between devices, padded(): lax.ppermute(head, axis, [((i + 1) % count, i) for i in range(ends)])  8.01 us
    dot_general x1, matrix products, per_device(): jnp.dot(one_hot.reshape(-1, land_count), settling_velocities, precision=l...  6.65 us
  transfers between devices with their start and end apart: 10, of which 4 were waited for; matrix products, arithmetic and copies ran while one was open for 9% of the time, Pallas kernels for 0%

profile of v1, /device:TPU:3, one launch (start us, length us, event | category | flops | bytes accessed | tf_op | source)
XLA Modules:
  0.0 151.7 jit_solution(5787807966658939250)
XLA Ops:
  0.6 0.0 copy-start
  0.6 0.9 copy.37
  1.5 0.9 copy.38
  2.4 0.9 copy.39
  3.3 0.9 copy.40
  4.2 0.8 pad_maximum_fusion.2
  5.0 4.6 %all-to-all-start = ((f32[8,64,128]{2,0,1:T(8,128)}), f32[8,64,128]{2,0,1:T(8,128)S(1)}, u32[]{:S(2)}, u32[]{:S(2)}) async-start(f32[8,64,128]{2,0,1:T(8,128)} %pad_maximum_fusion.2), calls=%async_computation | async-start | bytes 524288 | tf_op jit(solution)/shard_map/all_to_all | solution.py:99
  9.6 2.4 %fusion.48 = (bf16[2,3,512,128]{3,2,1,0:T(8,128)(2,1)}, bf16[2,3,512,128]{3,2,1,0:T(8,128)(2,1)S(1)}) fusion(bf16[2,16,512,128]{3,2,1,0:T(8,128)(2,1)} %param.13), kind=kLoop, calls=%fused_computation.97 | loop fusion | bytes 3145728 | tf_op jit(solution)/shard_map/slice | solution.py:17
  12.0 3.4 %collective-permute-start = (bf16[2,3,512,128]{3,2,1,0:T(8,128)(2,1)}, bf16[2,3,512,128]{3,2,1,0:T(8,128)(2,1)S(1)}, u32[]{:S(2)}, u32[]{:S(2)}) collective-permute-start(bf16[2,3,512,128]{3,2,1,0:T(8,128)(2,1)} %get-tuple-element.4), channel_id=1, source_target_pairs={{0,1},{1,2},{2,3},{3,4},{4,5},{5,6},{6,7},{7,8},{8,9},{9,10},{10,1... | collective-permute-start | bytes 2359304 | tf_op jit(solution)/shard_map/ppermute | solution.py:20
  15.4 4.8 %collective-permute-start.1 = (bf16[2,3,512,128]{3,2,1,0:T(8,128)(2,1)S(1)}, bf16[2,3,512,128]{3,2,1,0:T(8,128)(2,1)S(1)}, u32[]{:S(2)}, u32[]{:S(2)}) collective-permute-start(bf16[2,3,512,128]{3,2,1,0:T(8,128)(2,1)S(1)} %get-tuple-element.5), channel_id=1, source_target_pairs={{1,0},{2,1},{3,2},{4,3},{5,4},{6,5},{7,6},{8,7},{9,8},{10,9},{11,1... | collective-permute-start | bytes 2359304 | tf_op jit(solution)/shard_map/ppermute | solution.py:22
  20.2 0.1 slice.167
  20.3 0.1 slice.175
  20.4 0.1 slice.183
  20.4 0.8 convert_element_type.31
  21.3 0.8 fusion.30
  22.1 0.2 copy.52
  22.3 0.7 fusion.49
  23.0 0.1 slice.158
  23.0 0.6 fusion.50
  23.7 1.9 %collective-permute-start.2 = (f32[4,3,512]{2,1,0:T(4,128)}, f32[4,3,512]{2,1,0:T(4,128)S(1)}, u32[]{:S(2)}, u32[]{:S(2)}) collective-permute-start(f32[4,3,512]{2,1,0:T(4,128)} %get-tuple-element.24), channel_id=1, source_target_pairs={{0,1},{1,2},{2,3},{3,4},{4,5},{5,6},{6,7},{7,8},{8,9},{9,10},{10,1... | collective-permute-start | bytes 73736 | tf_op jit(solution)/shard_map/ppermute | solution.py:20
  25.6 5.4 %collective-permute-start.3 = (f32[4,3,512]{2,1,0:T(4,128)}, f32[4,3,512]{2,1,0:T(4,128)S(1)}, u32[]{:S(2)}, u32[]{:S(2)}) collective-permute-start(f32[4,3,512]{2,1,0:T(4,128)} %get-tuple-element.25), channel_id=1, source_target_pairs={{1,0},{2,1},{3,2},{4,3},{5,4},{6,5},{7,6},{8,7},{9,8},{10,9},{11,1... | collective-permute-start | bytes 73736 | tf_op jit(solution)/shard_map/ppermute | solution.py:22
  31.0 0.9 slice.197
  31.9 0.6 subtract_divide_fusion
  32.6 1.5 max.43
  34.0 0.6 max.45
  34.7 0.6 min.43
  35.3 0.7 min.45
  36.0 0.7 mul.235
  36.6 17.5 %collective-permute-done.2 = f32[4,3,512]{2,1,0:T(4,128)S(1)} collective-permute-done((f32[4,3,512]{2,1,0:T(4,128)}, f32[4,3,512]{2,1,0:T(4,128)S(1)}, u32[]{:S(2)}, u32[]{:S(2)}) %collective-permute-start.2) | collective-permute-done | bytes 24608 | tf_op jit(solution)/shard_map/ppermute | solution.py:20
  54.1 0.8 collective-permute-done.3
  55.0 0.7 slice_maximum_fusion.3
  55.7 0.7 slice_maximum_fusion.1
  56.4 3.5 %maximum_convert_fusion = f32[2,22,512,128]{3,2,1,0:T(8,128)S(1)} fusion(bf16[2,3,512,128]{3,2,1,0:T(8,128)(2,1)S(1)} %collective-permute-done.1, bf16[2,16,512,128]{3,2,1,0:T(8,128)(2,1)} %param.13, bf16[2,3,512,128]{3,2,1,0:T(8,128)(2,1)S(1)} %collective-permute-done), kind=kLoop, calls=%fused_computation.28 | loop fusion | flops 8650752 | bytes 17301504 | tf_op jit(solution)/shard_map/convert_element_type | solution.py:102
  59.9 4.7 %slice.203 = f32[2,20,512,128]{3,2,1,0:T(8,128)} slice(f32[2,22,512,128]{3,2,1,0:T(8,128)S(1)} %maximum_convert_fusion), slice={[0:2], [1:21], [0:512], [0:128]} | slice | bytes 20971520 | tf_op jit(solution)/shard_map/slice | solution.py:40
  64.7 15.4 %fusion.4 = f32[2,20,512,128]{3,2,1,0:T(8,128)} fusion(f32[2,20,512,128]{3,2,1,0:T(8,128)} %slice.203, f32[2,22,512,128]{3,2,1,0:T(8,128)S(1)} %maximum_convert_fusion, f32[20]{0:T(128)S(1)} %slice.167, f32[2,20,512]{2,1,0:T(8,128)S(1)} %copy-done.3, f32[2,20,512]{2,1,0:T(8,128)S(1)} %copy-done.4, f32[2,20,512]{2,1,0:T(8,128)S(1)} %get-tuple-element.21, ...), kind=kLoop, calls=%fused_computation.5 | loop fusion | flops 34078720 | bytes 42270800 | tf_op jit(solution)/shard_map/mul | solution.py:116
  80.1 3.7 %slice-done = f32[2,18,512,128]{3,2,1,0:T(8,128)S(1)} async-done(((f32[2,20,512,128]{3,2,1,0:T(8,128)}), f32[2,18,512,128]{3,2,1,0:T(8,128)S(1)}, s32[]{:S(2)}) %slice-start) | async-done | bytes 9437208 | tf_op jit(solution)/shard_map/slice | solution.py:40
  83.7 13.3 %fusion.11 = f32[2,18,512,128]{3,2,1,0:T(8,128)S(1)} fusion(f32[2,18,512,128]{3,2,1,0:T(8,128)S(1)} %slice-done, f32[2,20,512,128]{3,2,1,0:T(8,128)} %fusion.4, f32[18]{0:T(128)S(1)} %slice.175, f32[2,18,512]{2,1,0:T(8,128)} %get-tuple-element.18, f32[2,18,512]{2,1,0:T(8,128)} %get-tuple-element.19, f32[2,18,512]{2,1,0:T(8,128)S(1)} %get-tuple-element.17, ...), kind=kLoop, calls=%fused_computation.14 | loop fusion | flops 30670848 | bytes 38043720 | tf_op jit(solution)/shard_map/mul | solution.py:116
  97.0 0.6 slice.216
  97.6 0.2 copy-done.7
  97.8 0.0 copy-done.8
  97.9 0.0 copy-done.9
  97.9 0.0 copy-done.10
  97.9 10.9 %fusion.18 = f32[2,16,512,128]{3,2,1,0:T(8,128)} fusion(f32[2,16,512,128]{3,2,1,0:T(8,128)S(1)} %slice.216, f32[2,18,512,128]{3,2,1,0:T(8,128)S(1)} %fusion.11, f32[16]{0:T(128)S(1)} %slice.183, f32[2,16,512]{2,1,0:T(8,128)S(1)} %copy-done.10, f32[2,16,512]{2,1,0:T(8,128)S(1)} %copy-done.8, f32[2,16,512]{2,1,0:T(8,128)S(1)} %copy-done.9, ...), kind=kLoop, calls=%fused_computation.23 | loop fusion | flops 27262976 | bytes 33816640 | tf_op jit(solution)/shard_map/mul | solution.py:116
  108.8 3.4 %copy-done.2 = f32[2,16,512,128]{3,2,1,0:T(8,128)S(1)} copy-done((f32[2,16,512,128]{3,2,1,0:T(8,128)S(1)}, f32[2,16,512,128]{3,2,1,0:T(8,128)}, u32[]{:S(2)}) %copy-start.2) | copy-done | bytes 8388632
  112.2 6.6 %fusion.26 = f32[1,16,512,128]{3,2,1,0:T(8,128)} fusion(f32[2,16,512,128]{3,2,1,0:T(8,128)S(1)} %copy-done.2, f32[16,512]{1,0:T(8,128)S(1)} %bitcast.96, s32[16,512]{1,0:T(8,128)} %param.21, f32[24,128]{1,0:T(8,128)S(1)} %copy-done), kind=kOutput, calls=%fused_computation.37 | convolution fusion | flops 305332224 | bytes 8466432 | tf_op jit(solution)/shard_map/dot_general | solution.py:121
  118.9 3.5 %pad_maximum_fusion = f32[2,16,512,128]{3,2,1,0:T(8,128)S(1)} fusion(f32[1,16,512,128]{3,2,1,0:T(8,128)S(1)} %slice-done.1, f32[1,16,512,128]{3,2,1,0:T(8,128)} %fusion.26), kind=kLoop, calls=%fused_computation.27 | loop fusion | flops 2097152 | bytes 16777216 | tf_op jit(solution)/shard_map/concatenate | solution.py:125
  122.4 0.0 copy-start.1
  122.4 1.3 fusion.27
  123.7 2.1 %copy-done.1 = f32[2,16,512,128]{3,2,1,0:T(8,128)} copy-done((f32[2,16,512,128]{3,2,1,0:T(8,128)}, f32[2,16,512,128]{3,2,1,0:T(8,128)S(1)}, u32[]{:S(2)}) %copy-start.1) | copy-done | bytes 8388632
  125.8 1.4 fusion.24
  127.2 0.1 broadcast_multiply_fusion
  127.3 0.3 copy.44
  127.7 0.8 pad_maximum_fusion.1
  128.5 3.5 %all-to-all-start.1 = ((f32[4,16,16,128]{3,2,1,0:T(8,128)}), f32[4,16,16,128]{3,2,1,0:T(8,128)S(1)}, u32[]{:S(2)}, u32[]{:S(2)}) async-start(f32[4,16,16,128]{3,2,1,0:T(8,128)} %pad_maximum_fusion.1), calls=%async_computation.1 | async-start | bytes 1048576 | tf_op jit(solution)/shard_map/all_to_all | solution.py:143
  132.0 4.2 %collective-permute-start.4 = (bf16[2,1,128]{2,1,0:T(2,128)(2,1)S(1)}, bf16[2,1,128]{2,1,0:T(2,128)(2,1)S(1)}, u32[]{:S(2)}, u32[]{:S(2)}) collective-permute-start(bf16[2,1,128]{2,1,0:T(2,128)(2,1)S(1)} %get-tuple-element.30), channel_id=1, source_target_pairs={{0,4},{4,8},{8,12},{12,16},{16,20},{20,24},{24,28},{1,5},{5,9},{9,... | collective-permute-start | bytes 1544 | tf_op jit(solution)/shard_map/ppermute | solution.py:20
  136.2 1.9 %collective-permute-start.5 = (bf16[2,1,128]{2,1,0:T(2,128)(2,1)S(1)}, bf16[2,1,128]{2,1,0:T(2,128)(2,1)S(1)}, u32[]{:S(2)}, u32[]{:S(2)}) collective-permute-start(bf16[2,1,128]{2,1,0:T(2,128)(2,1)S(1)} %get-tuple-element.31), channel_id=1, source_target_pairs={{4,0},{8,4},{12,8},{16,12},{20,16},{24,20},{28,24},{5,1},{9,5},{13... | collective-permute-start | bytes 1544 | tf_op jit(solution)/shard_map/ppermute | solution.py:22
  138.1 3.9 %collective-permute-done.5 = bf16[2,1,128]{2,1,0:T(2,128)(2,1)S(1)} collective-permute-done((bf16[2,1,128]{2,1,0:T(2,128)(2,1)S(1)}, bf16[2,1,128]{2,1,0:T(2,128)(2,1)S(1)}, u32[]{:S(2)}, u32[]{:S(2)}) %collective-permute-start.5) | collective-permute-done | bytes 544 | tf_op jit(solution)/shard_map/ppermute | solution.py:22
  142.0 0.1 fusion.51
  142.1 3.9 %collective-permute-start.6 = (bf16[2,66,1]{2,1,0:T(8,128)(2,1)S(1)}, bf16[2,66,1]{2,1,0:T(8,128)(2,1)S(1)}, u32[]{:S(2)}, u32[]{:S(2)}) collective-permute-start(bf16[2,66,1]{2,1,0:T(8,128)(2,1)S(1)} %get-tuple-element.26), channel_id=1, source_target_pairs={{0,1},{1,2},{2,3},{4,5},{5,6},{6,7},{8,9},{9,10},{10,11},{12,13},{... | collective-permute-start | bytes 800 | tf_op jit(solution)/shard_map/ppermute | solution.py:20
  145.9 1.3 collective-permute-start.7
  147.3 3.4 %collective-permute-done.7 = bf16[2,66,1]{2,1,0:T(8,128)(2,1)S(1)} collective-permute-done((bf16[2,66,1]{2,1,0:T(8,128)(2,1)S(1)}, bf16[2,66,1]{2,1,0:T(8,128)(2,1)S(1)}, u32[]{:S(2)}, u32[]{:S(2)}) %collective-permute-start.7) | collective-permute-done | bytes 296 | tf_op jit(solution)/shard_map/ppermute | solution.py:22
  150.7 0.1 maximum_convert_fusion.1
  150.8 0.1 fusion.39
  151.0 0.8 fusion.43
  (44 shorter events, 0.3 us)
Async XLA Ops:
  0.6 108.2 %copy-start = (f32[24,128]{1,0:T(8,128)S(1)}, f32[24,128]{1,0:T(8,128)}, u32[]{:S(2)}) copy-start(f32[24,128]{1,0:T(8,128)} %param.24) | copy-start | bytes 36868
  5.0 17.0 %all-to-all-start = ((f32[8,64,128]{2,0,1:T(8,128)}), f32[8,64,128]{2,0,1:T(8,128)S(1)}, u32[]{:S(2)}, u32[]{:S(2)}) async-start(f32[8,64,128]{2,0,1:T(8,128)} %pad_maximum_fusion.2), calls=%async_computation | async-start | bytes 524288 | tf_op jit(solution)/shard_map/all_to_all | solution.py:99
  12.0 44.4 %collective-permute-start = (bf16[2,3,512,128]{3,2,1,0:T(8,128)(2,1)}, bf16[2,3,512,128]{3,2,1,0:T(8,128)(2,1)S(1)}, u32[]{:S(2)}, u32[]{:S(2)}) collective-permute-start(bf16[2,3,512,128]{3,2,1,0:T(8,128)(2,1)} %get-tuple-element.4), channel_id=1, source_target_pairs={{0,1},{1,2},{2,3},{3,4},{4,5},{5,6},{6,7},{7,8},{8,9},{9,10},{10,1... | collective-permute-start | bytes 2359304 | tf_op jit(solution)/shard_map/ppermute | solution.py:20
  15.4 41.0 %collective-permute-start.1 = (bf16[2,3,512,128]{3,2,1,0:T(8,128)(2,1)S(1)}, bf16[2,3,512,128]{3,2,1,0:T(8,128)(2,1)S(1)}, u32[]{:S(2)}, u32[]{:S(2)}) collective-permute-start(bf16[2,3,512,128]{3,2,1,0:T(8,128)(2,1)S(1)} %get-tuple-element.5), channel_id=1, source_target_pairs={{1,0},{2,1},{3,2},{4,3},{5,4},{6,5},{7,6},{8,7},{9,8},{10,9},{11,1... | collective-permute-start | bytes 2359304 | tf_op jit(solution)/shard_map/ppermute | solution.py:22
  23.7 30.4 %collective-permute-start.2 = (f32[4,3,512]{2,1,0:T(4,128)}, f32[4,3,512]{2,1,0:T(4,128)S(1)}, u32[]{:S(2)}, u32[]{:S(2)}) collective-permute-start(f32[4,3,512]{2,1,0:T(4,128)} %get-tuple-element.24), channel_id=1, source_target_pairs={{0,1},{1,2},{2,3},{3,4},{4,5},{5,6},{6,7},{7,8},{8,9},{9,10},{10,1... | collective-permute-start | bytes 73736 | tf_op jit(solution)/shard_map/ppermute | solution.py:20
  25.6 29.3 %collective-permute-start.3 = (f32[4,3,512]{2,1,0:T(4,128)}, f32[4,3,512]{2,1,0:T(4,128)S(1)}, u32[]{:S(2)}, u32[]{:S(2)}) collective-permute-start(f32[4,3,512]{2,1,0:T(4,128)} %get-tuple-element.25), channel_id=1, source_target_pairs={{1,0},{2,1},{3,2},{4,3},{5,4},{6,5},{7,6},{8,7},{9,8},{10,9},{11,1... | collective-permute-start | bytes 73736 | tf_op jit(solution)/shard_map/ppermute | solution.py:22
  59.9 4.7 %copy-start.3 = (f32[2,20,512]{2,1,0:T(8,128)S(1)}, f32[2,20,512]{2,1,0:T(8,128)}, u32[]{:S(2)}) copy-start(f32[2,20,512]{2,1,0:T(8,128)} %get-tuple-element.22) | copy-start | bytes 245764
  59.9 4.7 %copy-start.4 = (f32[2,20,512]{2,1,0:T(8,128)S(1)}, f32[2,20,512]{2,1,0:T(8,128)}, u32[]{:S(2)}) copy-start(f32[2,20,512]{2,1,0:T(8,128)} %get-tuple-element.23) | copy-start | bytes 245764
  80.0 3.7 %slice-start = ((f32[2,20,512,128]{3,2,1,0:T(8,128)}), f32[2,18,512,128]{3,2,1,0:T(8,128)S(1)}, s32[]{:S(2)}) async-start(f32[2,20,512,128]{3,2,1,0:T(8,128)} %fusion.4), calls=%async_computation.2 | async-start | bytes 18874368 | tf_op jit(solution)/shard_map/slice | solution.py:40
  97.0 0.8 copy-start.7
  97.0 0.9 copy-start.8
  97.0 0.9 copy-start.9
  97.0 0.9 copy-start.10
  108.8 3.4 %copy-start.2 = (f32[2,16,512,128]{3,2,1,0:T(8,128)S(1)}, f32[2,16,512,128]{3,2,1,0:T(8,128)}, u32[]{:S(2)}) copy-start(f32[2,16,512,128]{3,2,1,0:T(8,128)} %fusion.18) | copy-start | bytes 25165828
  112.2 6.7 %slice-start.1 = ((f32[2,16,512,128]{3,2,1,0:T(8,128)}), f32[1,16,512,128]{3,2,1,0:T(8,128)S(1)}, s32[]{:S(2)}) async-start(f32[2,16,512,128]{3,2,1,0:T(8,128)} %fusion.18), calls=%async_computation.3 | async-start | bytes 8388608 | tf_op jit(solution)/shard_map/slice | solution.py:126
  118.9 3.5 %copy-start.13 = (bf16[128,64]{0,1:T(8,128)(2,1)S(1)}, bf16[128,64]{0,1:T(8,128)(2,1)}, u32[]{:S(2)}) copy-start(bf16[128,64]{0,1:T(8,128)(2,1)} %param.23) | copy-start | bytes 49156
  118.9 3.5 %copy-start.14 = (bf16[128,64]{0,1:T(8,128)(2,1)S(1)}, bf16[128,64]{0,1:T(8,128)(2,1)}, u32[]{:S(2)}) copy-start(bf16[128,64]{0,1:T(8,128)(2,1)} %param.22) | copy-start | bytes 49156
  122.4 3.4 %copy-start.1 = (f32[2,16,512,128]{3,2,1,0:T(8,128)}, f32[2,16,512,128]{3,2,1,0:T(8,128)S(1)}, u32[]{:S(2)}) copy-start(f32[2,16,512,128]{3,2,1,0:T(8,128)S(1)} %pad_maximum_fusion) | copy-start | bytes 25165828
  122.4 3.4 %copy-start.6 = (f32[2,16,512]{2,1,0:T(8,128)S(1)}, f32[2,16,512]{2,1,0:T(8,128)}, u32[]{:S(2)}) copy-start(f32[2,16,512]{2,1,0:T(8,128)} %subtract_divide_fusion) | copy-start | bytes 196612
  125.8 1.4 copy-start.12
  125.8 21.5 %copy-start.5 = (f32[64,128]{1,0:T(8,128)S(1)}, f32[64,128]{1,0:T(8,128)}, u32[]{:S(2)}) copy-start(f32[64,128]{1,0:T(8,128)} %param.18) | copy-start | bytes 98308
  125.8 25.1 %copy-start.15 = (f32[4]{0:T(128)S(1)}, f32[4]{0:T(128)}, u32[]{:S(2)}) copy-start(f32[4]{0:T(128)} %param.25) | copy-start | bytes 52
  125.8 25.2 %copy-start.11 = (f32[2,64,128]{2,1,0:T(8,128)S(1)}, f32[2,64,128]{2,1,0:T(8,128)}, u32[]{:S(2)}) copy-start(f32[2,64,128]{2,1,0:T(8,128)} %param.19) | copy-start | bytes 196612
  128.5 22.3 %all-to-all-start.1 = ((f32[4,16,16,128]{3,2,1,0:T(8,128)}), f32[4,16,16,128]{3,2,1,0:T(8,128)S(1)}, u32[]{:S(2)}, u32[]{:S(2)}) async-start(f32[4,16,16,128]{3,2,1,0:T(8,128)} %pad_maximum_fusion.1), calls=%async_computation.1 | async-start | bytes 1048576 | tf_op jit(solution)/shard_map/all_to_all | solution.py:143
  132.0 6.1 %collective-permute-start.4 = (bf16[2,1,128]{2,1,0:T(2,128)(2,1)S(1)}, bf16[2,1,128]{2,1,0:T(2,128)(2,1)S(1)}, u32[]{:S(2)}, u32[]{:S(2)}) collective-permute-start(bf16[2,1,128]{2,1,0:T(2,128)(2,1)S(1)} %get-tuple-element.30), channel_id=1, source_target_pairs={{0,4},{4,8},{8,12},{12,16},{16,20},{20,24},{24,28},{1,5},{5,9},{9,... | collective-permute-start | bytes 1544 | tf_op jit(solution)/shard_map/ppermute | solution.py:20
  136.2 5.8 %collective-permute-start.5 = (bf16[2,1,128]{2,1,0:T(2,128)(2,1)S(1)}, bf16[2,1,128]{2,1,0:T(2,128)(2,1)S(1)}, u32[]{:S(2)}, u32[]{:S(2)}) collective-permute-start(bf16[2,1,128]{2,1,0:T(2,128)(2,1)S(1)} %get-tuple-element.31), channel_id=1, source_target_pairs={{4,0},{8,4},{12,8},{16,12},{20,16},{24,20},{28,24},{5,1},{9,5},{13... | collective-permute-start | bytes 1544 | tf_op jit(solution)/shard_map/ppermute | solution.py:22
  142.1 5.2 %collective-permute-start.6 = (bf16[2,66,1]{2,1,0:T(8,128)(2,1)S(1)}, bf16[2,66,1]{2,1,0:T(8,128)(2,1)S(1)}, u32[]{:S(2)}, u32[]{:S(2)}) collective-permute-start(bf16[2,66,1]{2,1,0:T(8,128)(2,1)S(1)} %get-tuple-element.26), channel_id=1, source_target_pairs={{0,1},{1,2},{2,3},{4,5},{5,6},{6,7},{8,9},{9,10},{10,11},{12,13},{... | collective-permute-start | bytes 800 | tf_op jit(solution)/shard_map/ppermute | solution.py:20
  145.9 4.7 %collective-permute-start.7 = (bf16[2,66,1]{2,1,0:T(8,128)(2,1)S(1)}, bf16[2,66,1]{2,1,0:T(8,128)(2,1)S(1)}, u32[]{:S(2)}, u32[]{:S(2)}) collective-permute-start(bf16[2,66,1]{2,1,0:T(8,128)(2,1)S(1)} %get-tuple-element.27), channel_id=1, source_target_pairs={{1,0},{2,1},{3,2},{5,4},{6,5},{7,6},{9,8},{10,9},{11,10},{13,12},{... | collective-permute-start | bytes 800 | tf_op jit(solution)/shard_map/ppermute | solution.py:22
